TPU v7x, 32 devices: a whole 2x2x4 slice. The times are simulated.
32 devices in a mesh: row: 8 (over z, y), col: 4 (over x, core).
Axes of the slice: x: 2, y: 2, z: 4, core: 2. Of those that a mesh axis runs over, the one named last changes fastest.
Arguments:
- points: float32 [8, 5120], P(None, ('row', 'col')), may hold values from -6 to 6
- sketch: bfloat16 [5120, 256], P(('row', 'col')), may hold values from -0.625 to 0.625
- rank: int32 [5120], P(('row', 'col')), may hold values from 0 to 5119, each once
- boundary: int32 [1], replicated, may hold values from 1280 to 3840
- scales: float32 [8], replicated, may hold values from 1.5 to 4
Outputs:
- basis: float32 [5120, 256], P(('row', 'col'))
- factor: float32 [256, 256], replicated
Inputs may be any that keep to these rules, and one draw needn't show every extreme that they name: `rank`: each tree position appears once.
All inputs are finite; a program needn't handle non-finite values.
Results may differ from a plain program's by a relative error of at most 0.0006.
The roundings to bfloat16 on the way count: a program that leaves them out, or rounds other values in their place, can miss the bound.
Values may be sent and summed in bfloat16 or wider, within the bound.
A program may use at most 64 MiB of HBM per device.

v0:
```python
import jax
import jax.numpy as jnp
from jax import lax
from jax.sharding import PartitionSpec as P


def partial_terms(tgt_pts, tgt_side, src_pts, src_side, src_tests):
    total = src_pts.shape[1]
    blocks = total // total
    ranks = src_tests.shape[1]

    def term(start, count):
        tsq = jnp.sum(tgt_pts * tgt_pts, axis=0)

        def add_block(index, acc):
            ssq = jnp.sum(src_pts * src_pts, axis=0)
            inner = lax.dot_general(
                tgt_pts,
                src_pts,
                (((0,), (0,)), ((), ())),
                precision=lax.Precision.HIGHEST,
                preferred_element_type=jnp.float32,
            )
            dist = tsq[:, None] + ssq[None, :] - 2.0 * inner
            mask = (
                tgt_side[:, None] + src_side[None, :] - 2.0 * tgt_side[:, None] * src_side[None, :]
            )
            tile = (jnp.exp(-0.5 * dist) * mask).astype(jnp.bfloat16)
            return acc + jnp.dot(tile, src_tests, preferred_element_type=jnp.float32)

        return lax.fori_loop(0, blocks, add_block, jnp.zeros((count, ranks), jnp.float32))

    return term


def body(points, sketch, rank, boundary, scales):
    scaled = points / scales[:, None]
    side = (rank >= boundary[0]).astype(jnp.float32)
    local = points.shape[1]
    ranks = sketch.shape[1]
    everyone = lax.axis_size("row") * lax.axis_size("col") * local
    tgt_pts, tgt_side = (
        lax.all_gather(scaled, "col", axis=1, tiled=True),
        lax.all_gather(side, "col", axis=0, tiled=True),
    )
    src_pts, src_side = (
        lax.all_gather(scaled, "row", axis=1, tiled=True),
        lax.all_gather(side, "row", axis=0, tiled=True),
    )
    src_tests = lax.all_gather(sketch, "row", axis=0, tiled=True)
    term = partial_terms(tgt_pts, tgt_side, src_pts, src_side, src_tests)
    sample = lax.psum_scatter(
        term(jnp.int32(0), local * lax.axis_size("col")), "col", scatter_dimension=0, tiled=True
    )
    own_gram = jnp.dot(
        sample.T, sample, precision=lax.Precision.HIGHEST, preferred_element_type=jnp.float32
    )
    gram = lax.psum(own_gram, ("row", "col")) / jnp.float32(everyone)
    shift = 0.1 * jnp.trace(gram) / jnp.float32(ranks)
    factor = jnp.linalg.cholesky(gram + shift * jnp.eye(ranks, dtype=jnp.float32))
    basis = jax.scipy.linalg.solve_triangular(factor, sample.T, lower=True).T
    return (basis, factor)


def solution(mesh):
    placed = (P(None, ("row", "col")), P(("row", "col"), None), P(("row", "col")), P(), P())
    return jax.shard_map(
        body, mesh=mesh, in_specs=placed, out_specs=(P(("row", "col"), None), P()), check_vma=False
    )
```

profile of v0, /device:TPU:0, one launch (start us, length us, event | category | flops | bytes accessed | tf_op | source)
XLA Modules:
  0.0 342.7 jit_solution(11203993560195259603)
XLA Ops:
  8.0 32.3 %all-gather.1 = f32[8,160,8]{1,2,0:T(8,128)S(1)} all-gather(f32[1,160,8]{1,2,0:T(8,128)S(1)} %divide_bitcast_fusion), channel_id=1, replica_groups=mesh['row'=8,'col'=4] {'row'}, dimensions={0}, use_global_device_ids=true | all-gather | bytes 46080 | tf_op jit(solution)/shard_map/all_gather | solution.py:47
  40.3 5.2 %all-gather = f32[4,160,8]{1,2,0:T(8,128)S(1)} all-gather(f32[1,160,8]{1,2,0:T(8,128)S(1)} %divide_bitcast_fusion), channel_id=1, replica_groups=mesh['row'=8,'col'=4] {'col'}, dimensions={0}, use_global_device_ids=true | all-gather | bytes 25600 | tf_op jit(solution)/shard_map/all_gather | solution.py:43
  45.5 1.2 dynamic-slice.3
  46.7 1.2 dynamic-slice.4
  49.9 0.8 fusion.14
  50.8 7.1 %all-reduce.1 = f32[640]{0:T(1024)S(1)} all-reduce(f32[640]{0:T(1024)S(1)} %get-tuple-element.67), channel_id=1, replica_groups=mesh['row'=8,'col'=4] {'col'}, use_global_device_ids=true, to_apply=%add.1 | all-reduce | flops 640 | bytes 5120
  57.9 21.7 %all-reduce.2 = f32[1280]{0:T(1024)S(1)} all-reduce(f32[1280]{0:T(1024)S(1)} %get-tuple-element.66), channel_id=1, replica_groups=mesh['row'=8,'col'=4] {'row'}, use_global_device_ids=true, to_apply=%add.2 | all-reduce | flops 1280 | bytes 10240
  79.8 32.1 %all_gather.19 = bf16[1280,256]{1,0:T(8,128)(2,1)S(1)} all-gather(bf16[160,256]{1,0:T(8,128)(2,1)} %param.6), channel_id=1, replica_groups=mesh['row'=8,'col'=4] {'row'}, dimensions={0}, use_global_device_ids=true | all-gather | bytes 737280 | tf_op jit(solution)/shard_map/all_gather | solution.py:50
  112.0 3.7 %fusion.4 = bf16[640,1280]{1,0:T(8,128)(2,1)S(1)} fusion(f32[640,8]{0,1:T(8,128)S(1)} %reshape.56, f32[1280,8]{0,1:T(8,128)S(1)} %reshape.58, f32[640]{0:T(1024)S(1)} %broadcast_multiply_fusion, f32[1280]{0:T(1024)S(1)} %all-reduce.2, f32[640]{0:T(1024)S(1)} %all-reduce.1, f32[1280]{0:T(1024)S(1)} %multiply_reduce_fusion, f32[640]{0:T(1024)S(1)} %multiply_reduce_fusion.1), kind=kOutput, calls=%fused_computation.7 | convolution fusion | flops 86016000 | bytes 1717760 | tf_op jit(solution)/shard_map/while/body/eval_jaxpr/dot_general | solution.py:17
  115.6 1.4 fusion.17
  117.3 18.7 %reduce-scatter.2.cloned.1.call-done = f32[160,256]{1,0:T(8,128)} async-done(((f32[640,256]{1,0:T(8,128)}), f32[160,256]{1,0:T(8,128)}) %reduce-scatter.2.cloned.1.call-update) | async-done | bytes 163856 | tf_op jit(solution)/shard_map/reduce_scatter | solution.py:52
  136.0 2.4 fusion.18
  138.4 130.4 %all-reduce.5.cloned.1.call-done = f32[256,256]{0,1:T(8,128)} async-done(((f32[256,256]{0,1:T(8,128)}), f32[256,256]{0,1:T(8,128)}) %all-reduce.5.cloned.1.call-update) | async-done | bytes 262160 | tf_op jit(solution)/shard_map/psum | solution.py:58
  268.8 1.6 select_reduce_fusion
  271.0 1.0 select_add_fusion
  272.1 1.0 fusion.5
  273.1 11.7 %cholesky.49 = f32[128,128]{1,0:T(8,128)S(1)} custom-call(f32[128,128]{1,0:T(8,128)S(1)} %cholesky.115), custom_call_target="Cholesky" | custom-call | tf_op jit(solution)/shard_map/jit(cholesky)/cholesky | solution.py:60
  284.9 9.8 %custom-call.15 = f32[1,128,128]{1,2,0:T(8,128)S(1)} custom-call(f32[1,128,128]{2,1,0:T(8,128)S(1)} %get-tuple-element.65), custom_call_target="InvertDiagBlocksLowerTriangular" | custom-call | tf_op jit(solution)/shard_map/jit(cholesky)/cholesky | solution.py:60
  295.2 11.7 %cholesky.103 = f32[128,128]{1,0:T(8,128)S(1)} custom-call(f32[128,128]{1,0:T(8,128)S(1)} %convolution_subtract_fusion.1), custom_call_target="Cholesky" | custom-call | tf_op jit(solution)/shard_map/jit(cholesky)/cholesky | solution.py:60
  309.5 4.5 %while.1 = (s32[]{:T(128)}, f32[256,256]{0,1:T(8,128)S(1)}, s32[2,2]{1,0:T(2,128)S(1)}, f32[2,128,128]{2,1,0:T(8,128)S(1)}, s32[]{:T(128)}) while((s32[]{:T(128)}, f32[256,256]{0,1:T(8,128)S(1)}, s32[2,2]{1,0:T(2,128)S(1)}, f32[2,128,128]{2,1,0:T(8,128)S(1)}, s32[]{:T(128)}) %tuple.35), condition=%wide.while_cond, body=%wide.while_body.sunk | while | flops 2 | bytes 393321 | solution.py:61
  310.3 1.4 dynamic-slice.9
  312.5 1.4 dynamic-slice.9
  314.0 19.7 %custom-call.16 = f32[2,128,128]{1,2,0:T(8,128)S(1)} custom-call(f32[2,128,128]{2,1,0:T(8,128)S(1)} %get-tuple-element.33), custom_call_target="InvertDiagBlocksLowerTriangular" | custom-call | tf_op jit(solution)/shard_map/jit(_solve_triangular)/triangular_solve | solution.py:61
  335.1 0.8 copy.31
  (45 shorter events, 5.9 us)
Async XLA Ops:
  7.2 128.8 %reduce-scatter.2.cloned.1.call-start = ((), (), s32[]{:S(2)}) async-start(), calls=%async_computation.1 | async-start | bytes 819200 | tf_op jit(solution)/shard_map/reduce_scatter | solution.py:52
  117.1 151.7 %all-reduce.5.cloned.1.call-start = ((), (), s32[]{:S(2)}) async-start(), calls=%async_computation.2 | async-start | bytes 524288 | tf_op jit(solution)/shard_map/psum | solution.py:58
  307.3 26.4 %copy-start = (f32[160,256]{1,0:T(8,128)S(1)}, f32[160,256]{1,0:T(8,128)}, u32[]{:S(2)}) copy-start(f32[160,256]{1,0:T(8,128)} %reduce-scatter.2.cloned.1.call-done) | copy-start | bytes 491524
Sparse Core Ops, SparseCore 0:
  117.2 18.7 reduce-scatter.1
  142.0 126.6 all-reduce.4
where the time goes:
time: 343 us
  waiting for transfers between devices  149 us (43%)
  blocking collectives  98.4 us (29%)
  other arithmetic  59.6 us (17%)
  between operations  18.2 us (5%)
  matrix products  8.59 us (3%)
  local copies, waits for them, and re-layouts  8.31 us (2%)
    psum x1, waiting for transfers between devices, body(): gram = lax.psum(own_gram, ('row', 'col')) / jnp.float32(everyone)  130 us
    another operation x6, other arithmetic, body(): jnp.linalg.cholesky(gram + shift * jnp.eye(ranks, dtype=jnp.float32))  34 us
    all_gather x1, blocking collectives, body(): lax.all_gather(scaled, 'row', axis=1, tiled=True)  32.3 us
    all_gather x1, blocking collectives, body(): src_tests = lax.all_gather(sketch, 'row', axis=0, tiled=True)  32.1 us
    unnamed x2, blocking collectives  28.8 us
    another operation x3, other arithmetic, body(): basis = jax.scipy.linalg.solve_triangular(factor, sample.T, lower=True).T  19.7 us
    reduce_scatter x1, waiting for transfers between devices, body(): lax.psum_scatter(term(jnp.int32(0), local * lax.axis_size('col')), 'col',...  18.7 us
  transfers between devices with their start and end apart: 2, of which 2 were waited for; matrix products, arithmetic and copies ran while one was open for 0% of the time, Pallas kernels for 0%

commit v1 on v0

--- a/solution.py
+++ b/solution.py
@@ -55,7 +55,7 @@
     own_gram = jnp.dot(
         sample.T, sample, precision=lax.Precision.HIGHEST, preferred_element_type=jnp.float32
     )
-    gram = lax.psum(own_gram, ("row", "col")) / jnp.float32(everyone)
+    gram = lax.psum(lax.psum(own_gram, "row"), "col") / jnp.float32(everyone)
     shift = 0.1 * jnp.trace(gram) / jnp.float32(ranks)
     factor = jnp.linalg.cholesky(gram + shift * jnp.eye(ranks, dtype=jnp.float32))
     basis = jax.scipy.linalg.solve_triangular(factor, sample.T, lower=True).T

time: 343 us -> 319 us (0.930)
  waiting for transfers between devices: 149 us -> 125 us
    psum x1 -> x2, waiting for transfers between devices: 130 us -> 106 us  [body(): gram = lax.psum(lax.psum(own_gram, 'row'), 'col') / jnp.float32(everyone)]
  transfers between devices with their start and end apart: 2 -> 3, of which waited for: 2 -> 3; matrix products, arithmetic and copies ran while one was open for 0% -> 0% of each run, Pallas kernels for 0% -> 0%
where the time goes in v1:
time: 319 us; the launch traced here: 318 us
  waiting for transfers between devices  125 us (39%)
  blocking collectives  98.4 us (31%)
  other arithmetic  59.6 us (19%)
  between operations  17.9 us (6%)
  matrix products  8.6 us (3%)
  local copies, waits for them, and re-layouts  8.31 us (3%)
    psum x2, waiting for transfers between devices, body(): gram = lax.psum(lax.psum(own_gram, 'row'), 'col') / jnp.float32(everyone)  106 us
    another operation x6, other arithmetic, body(): jnp.linalg.cholesky(gram + shift * jnp.eye(ranks, dtype=jnp.float32))  34 us
    all_gather x1, blocking collectives, body(): lax.all_gather(scaled, 'row', axis=1, tiled=True)  32.3 us
    all_gather x1, blocking collectives, body(): src_tests = lax.all_gather(sketch, 'row', axis=0, tiled=True)  32.1 us
    unnamed x2, blocking collectives  28.8 us
    another operation x3, other arithmetic, body(): basis = jax.scipy.linalg.solve_triangular(factor, sample.T, lower=True).T  19.7 us
    reduce_scatter x1, waiting for transfers between devices, body(): lax.psum_scatter(term(jnp.int32(0), local * lax.axis_size('col')), 'col',...  18.8 us
  transfers between devices with their start and end apart: 3, of which 3 were waited for; matrix products, arithmetic and copies ran while one was open for 0% of the time, Pallas kernels for 0%

profile of v1, /device:TPU:0, one launch (start us, length us, event | category | flops | bytes accessed | tf_op | source)
XLA Modules:
  0.0 318.5 jit_solution(8639372183222740446)
XLA Ops:
  8.0 32.3 %all-gather.1 = f32[8,160,8]{1,2,0:T(8,128)S(1)} all-gather(f32[1,160,8]{1,2,0:T(8,128)S(1)} %divide_bitcast_fusion), channel_id=1, replica_groups=mesh['row'=8,'col'=4] {'row'}, dimensions={0}, use_global_device_ids=true | all-gather | bytes 46080 | tf_op jit(solution)/shard_map/all_gather | solution.py:47
  40.3 5.2 %all-gather = f32[4,160,8]{1,2,0:T(8,128)S(1)} all-gather(f32[1,160,8]{1,2,0:T(8,128)S(1)} %divide_bitcast_fusion), channel_id=1, replica_groups=mesh['row'=8,'col'=4] {'col'}, dimensions={0}, use_global_device_ids=true | all-gather | bytes 25600 | tf_op jit(solution)/shard_map/all_gather | solution.py:43
  45.5 1.2 dynamic-slice.3
  46.7 1.2 dynamic-slice.4
  50.8 7.1 %all-reduce.1 = f32[640]{0:T(1024)S(1)} all-reduce(f32[640]{0:T(1024)S(1)} %get-tuple-element.67), channel_id=1, replica_groups=mesh['row'=8,'col'=4] {'col'}, use_global_device_ids=true, to_apply=%add.1 | all-reduce | flops 640 | bytes 5120
  57.9 21.7 %all-reduce.2 = f32[1280]{0:T(1024)S(1)} all-reduce(f32[1280]{0:T(1024)S(1)} %get-tuple-element.66), channel_id=1, replica_groups=mesh['row'=8,'col'=4] {'row'}, use_global_device_ids=true, to_apply=%add.2 | all-reduce | flops 1280 | bytes 10240
  79.8 32.1 %all_gather.19 = bf16[1280,256]{1,0:T(8,128)(2,1)S(1)} all-gather(bf16[160,256]{1,0:T(8,128)(2,1)} %param.6), channel_id=1, replica_groups=mesh['row'=8,'col'=4] {'row'}, dimensions={0}, use_global_device_ids=true | all-gather | bytes 737280 | tf_op jit(solution)/shard_map/all_gather | solution.py:50
  112.0 3.7 %fusion.4 = bf16[640,1280]{1,0:T(8,128)(2,1)S(1)} fusion(f32[640,8]{0,1:T(8,128)S(1)} %reshape.56, f32[1280,8]{0,1:T(8,128)S(1)} %reshape.58, f32[640]{0:T(1024)S(1)} %broadcast_multiply_fusion, f32[1280]{0:T(1024)S(1)} %all-reduce.2, f32[640]{0:T(1024)S(1)} %all-reduce.1, f32[1280]{0:T(1024)S(1)} %multiply_reduce_fusion, f32[640]{0:T(1024)S(1)} %multiply_reduce_fusion.1), kind=kOutput, calls=%fused_computation.7 | convolution fusion | flops 86016000 | bytes 1717760 | tf_op jit(solution)/shard_map/while/body/eval_jaxpr/dot_general | solution.py:17
  115.6 1.4 fusion.17
  117.1 18.8 %reduce-scatter.2.cloned.1.call-done = f32[160,256]{1,0:T(8,128)} async-done(((f32[640,256]{1,0:T(8,128)}), f32[160,256]{1,0:T(8,128)}) %reduce-scatter.2.cloned.1.call-update) | async-done | bytes 163856 | tf_op jit(solution)/shard_map/reduce_scatter | solution.py:52
  136.0 2.4 fusion.18
  138.6 72.4 %all-reduce.6.cloned.1.call-done = f32[256,256]{0,1:T(8,128)} async-done(((f32[256,256]{0,1:T(8,128)}), f32[256,256]{0,1:T(8,128)}) %all-reduce.6.cloned.1.call-update) | async-done | bytes 262160 | tf_op jit(solution)/shard_map/psum | solution.py:58
  211.0 33.8 %all-reduce.8.cloned.1.call-done = f32[256,256]{0,1:T(8,128)} async-done(((f32[256,256]{0,1:T(8,128)}), f32[256,256]{0,1:T(8,128)}) %all-reduce.8.cloned.1.call-update) | async-done | bytes 262160 | tf_op jit(solution)/shard_map/psum | solution.py:58
  244.8 1.6 select_reduce_fusion
  247.0 1.0 select_add_fusion
  248.2 1.0 fusion.5
  249.2 11.7 %cholesky.49 = f32[128,128]{1,0:T(8,128)S(1)} custom-call(f32[128,128]{1,0:T(8,128)S(1)} %cholesky.115), custom_call_target="Cholesky" | custom-call | tf_op jit(solution)/shard_map/jit(cholesky)/cholesky | solution.py:60
  260.9 9.8 %custom-call.15 = f32[1,128,128]{1,2,0:T(8,128)S(1)} custom-call(f32[1,128,128]{2,1,0:T(8,128)S(1)} %get-tuple-element.65), custom_call_target="InvertDiagBlocksLowerTriangular" | custom-call | tf_op jit(solution)/shard_map/jit(cholesky)/cholesky | solution.py:60
  271.2 11.7 %cholesky.103 = f32[128,128]{1,0:T(8,128)S(1)} custom-call(f32[128,128]{1,0:T(8,128)S(1)} %convolution_subtract_fusion.1), custom_call_target="Cholesky" | custom-call | tf_op jit(solution)/shard_map/jit(cholesky)/cholesky | solution.py:60
  285.5 4.5 %while.1 = (s32[]{:T(128)}, f32[256,256]{0,1:T(8,128)S(1)}, s32[2,2]{1,0:T(2,128)S(1)}, f32[2,128,128]{2,1,0:T(8,128)S(1)}, s32[]{:T(128)}) while((s32[]{:T(128)}, f32[256,256]{0,1:T(8,128)S(1)}, s32[2,2]{1,0:T(2,128)S(1)}, f32[2,128,128]{2,1,0:T(8,128)S(1)}, s32[]{:T(128)}) %tuple.35), condition=%wide.while_cond, body=%wide.while_body.sunk | while | flops 2 | bytes 393321 | solution.py:61
  286.3 1.4 dynamic-slice.9
  288.5 1.4 dynamic-slice.9
  290.0 19.7 %custom-call.16 = f32[2,128,128]{1,2,0:T(8,128)S(1)} custom-call(f32[2,128,128]{2,1,0:T(8,128)S(1)} %get-tuple-element.33), custom_call_target="InvertDiagBlocksLowerTriangular" | custom-call | tf_op jit(solution)/shard_map/jit(_solve_triangular)/triangular_solve | solution.py:61
  311.1 0.8 copy.31
  (48 shorter events, 6.8 us)
Async XLA Ops:
  7.2 128.8 %reduce-scatter.2.cloned.1.call-start = ((), (), s32[]{:S(2)}) async-start(), calls=%async_computation.1 | async-start | bytes 819200 | tf_op jit(solution)/shard_map/reduce_scatter | solution.py:52
  117.1 93.9 %all-reduce.6.cloned.1.call-start = ((), (), s32[]{:S(2)}) async-start(), calls=%async_computation.2 | async-start | bytes 524288 | tf_op jit(solution)/shard_map/psum | solution.py:58
  138.3 106.4 %all-reduce.8.cloned.1.call-start = ((), (), s32[]{:S(2)}) async-start(), calls=%async_computation.3 | async-start | bytes 524288 | tf_op jit(solution)/shard_map/psum | solution.py:58
  283.3 26.4 %copy-start = (f32[160,256]{1,0:T(8,128)S(1)}, f32[160,256]{1,0:T(8,128)}, u32[]{:S(2)}) copy-start(f32[160,256]{1,0:T(8,128)} %reduce-scatter.2.cloned.1.call-done) | copy-start | bytes 491524
Sparse Core Ops, SparseCore 0:
  117.2 18.7 reduce-scatter.1
  139.9 71.0 all-reduce.5
  213.3 31.4 all-reduce.7

commit v2 on v0

--- a/solution.py
+++ b/solution.py
@@ -55,7 +55,7 @@
     own_gram = jnp.dot(
         sample.T, sample, precision=lax.Precision.HIGHEST, preferred_element_type=jnp.float32
     )
-    gram = lax.psum(own_gram, ("row", "col")) / jnp.float32(everyone)
+    gram = jnp.sum(lax.all_gather(own_gram, ("row", "col")), axis=0) / jnp.float32(everyone)
     shift = 0.1 * jnp.trace(gram) / jnp.float32(ranks)
     factor = jnp.linalg.cholesky(gram + shift * jnp.eye(ranks, dtype=jnp.float32))
     basis = jax.scipy.linalg.solve_triangular(factor, sample.T, lower=True).T

time: 343 us -> 291 us (0.85)
  waiting for transfers between devices: 149 us -> 96.8 us
    psum x1 -> x0, waiting for transfers between devices: 130 us -> none  [body(): gram = lax.psum(own_gram, ('row', 'col')) / jnp.float32(everyone)]
    all_gather x0 -> x1, waiting for transfers between devices: none -> 78.1 us  [body(): lax.all_gather(own_gram, ('row', 'col'))]
    reduce_sum x0 -> x1, other arithmetic: none -> 3.93 us  [body(): jnp.sum(lax.all_gather(own_gram, ('row', 'col')), axis=0)]
where the time goes in v2:
time: 291 us
  blocking collectives  98.4 us (34%)
  waiting for transfers between devices  96.8 us (33%)
  other arithmetic  61.4 us (21%)
  between operations  18.1 us (6%)
  matrix products  8.64 us (3%)
  local copies, waits for them, and re-layouts  6.94 us (2%)
    all_gather x1, waiting for transfers between devices, body(): lax.all_gather(own_gram, ('row', 'col'))  78.1 us
    another operation x6, other arithmetic, body(): jnp.linalg.cholesky(gram + shift * jnp.eye(ranks, dtype=jnp.float32))  34 us
    all_gather x1, blocking collectives, body(): lax.all_gather(scaled, 'row', axis=1, tiled=True)  32.3 us
    all_gather x1, blocking collectives, body(): src_tests = lax.all_gather(sketch, 'row', axis=0, tiled=True)  32.1 us
    unnamed x2, blocking collectives  28.8 us
    another operation x3, other arithmetic, body(): basis = jax.scipy.linalg.solve_triangular(factor, sample.T, lower=True).T  20.4 us
    reduce_scatter x1, waiting for transfers between devices, body(): lax.psum_scatter(term(jnp.int32(0), local * lax.axis_size('col')), 'col',...  18.7 us
  transfers between devices with their start and end apart: 2, of which 2 were waited for; matrix products, arithmetic and copies ran while one was open for 0% of the time, Pallas kernels for 0%

profile of v2, /device:TPU:0, one launch (start us, length us, event | category | flops | bytes accessed | tf_op | source)
XLA Modules:
  0.0 290.6 jit_solution(3791945292188285604)
XLA Ops:
  7.2 0.8 divide_bitcast_fusion
  8.0 32.3 %all-gather.2 = f32[8,160,8]{1,2,0:T(8,128)S(1)} all-gather(f32[1,160,8]{1,2,0:T(8,128)S(1)} %divide_bitcast_fusion), channel_id=1, replica_groups=mesh['row'=8,'col'=4] {'row'}, dimensions={0}, use_global_device_ids=true | all-gather | bytes 46080 | tf_op jit(solution)/shard_map/all_gather | solution.py:47
  40.3 5.2 %all-gather.1 = f32[4,160,8]{1,2,0:T(8,128)S(1)} all-gather(f32[1,160,8]{1,2,0:T(8,128)S(1)} %divide_bitcast_fusion), channel_id=1, replica_groups=mesh['row'=8,'col'=4] {'col'}, dimensions={0}, use_global_device_ids=true | all-gather | bytes 25600 | tf_op jit(solution)/shard_map/all_gather | solution.py:43
  45.5 1.2 dynamic-slice.3
  46.7 1.2 dynamic-slice.4
  49.9 0.8 fusion.13
  50.8 7.1 %all-reduce.1 = f32[640]{0:T(1024)S(1)} all-reduce(f32[640]{0:T(1024)S(1)} %get-tuple-element.53), channel_id=1, replica_groups=mesh['row'=8,'col'=4] {'col'}, use_global_device_ids=true, to_apply=%add.1 | all-reduce | flops 640 | bytes 5120
  57.9 21.7 %all-reduce.2 = f32[1280]{0:T(1024)S(1)} all-reduce(f32[1280]{0:T(1024)S(1)} %get-tuple-element.52), channel_id=1, replica_groups=mesh['row'=8,'col'=4] {'row'}, use_global_device_ids=true, to_apply=%add.2 | all-reduce | flops 1280 | bytes 10240
  79.8 32.1 %all_gather.25 = bf16[1280,256]{1,0:T(8,128)(2,1)S(1)} all-gather(bf16[160,256]{1,0:T(8,128)(2,1)} %param.6), channel_id=1, replica_groups=mesh['row'=8,'col'=4] {'row'}, dimensions={0}, use_global_device_ids=true | all-gather | bytes 737280 | tf_op jit(solution)/shard_map/all_gather | solution.py:50
  112.0 3.7 %fusion.4 = bf16[640,1280]{1,0:T(8,128)(2,1)S(1)} fusion(f32[640,8]{0,1:T(8,128)S(1)} %reshape.57, f32[1280,8]{0,1:T(8,128)S(1)} %reshape.59, f32[640]{0:T(1024)S(1)} %broadcast_multiply_fusion, f32[1280]{0:T(1024)S(1)} %all-reduce.2, f32[640]{0:T(1024)S(1)} %all-reduce.1, f32[1280]{0:T(1024)S(1)} %multiply_reduce_fusion, f32[640]{0:T(1024)S(1)} %multiply_reduce_fusion.1), kind=kOutput, calls=%fused_computation.7 | convolution fusion | flops 86016000 | bytes 1717760 | tf_op jit(solution)/shard_map/while/body/eval_jaxpr/dot_general | solution.py:17
  115.6 1.4 fusion.16
  117.3 18.7 %reduce-scatter.2.cloned.1.call-done = f32[160,256]{1,0:T(8,128)} async-done(((f32[640,256]{1,0:T(8,128)}), f32[160,256]{1,0:T(8,128)}) %reduce-scatter.2.cloned.1.call-update) | async-done | bytes 163856 | tf_op jit(solution)/shard_map/reduce_scatter | solution.py:52
  136.0 2.4 fusion.17
  138.4 78.1 %all-gather.5.cloned.1.call-done = f32[8192,256]{1,0:T(8,128)} async-done(((f32[256,256]{1,0:T(8,128)}), f32[8192,256]{1,0:T(8,128)}) %all-gather.5.cloned.1.call-update) | async-done | bytes 8388624 | tf_op jit(solution)/shard_map/all_gather | solution.py:58
  216.5 3.9 %reduce_sum.40 = f32[256,256]{1,0:T(8,128)S(1)} reduce(f32[32,256,256]{2,1,0:T(8,128)} %bitcast.51, f32[]{:T(128)} %constant.98.clone.1), dimensions={0}, to_apply=%region_3.0 | reduce | flops 2031616 | bytes 8650756 | tf_op jit(solution)/shard_map/reduce_sum | solution.py:58
  221.9 11.7 %cholesky.49 = f32[128,128]{1,0:T(8,128)S(1)} custom-call(f32[128,128]{1,0:T(8,128)S(1)} %cholesky.115), custom_call_target="Cholesky" | custom-call | tf_op jit(solution)/shard_map/jit(cholesky)/cholesky | solution.py:60
  233.7 9.8 %custom-call.15 = f32[1,128,128]{1,2,0:T(8,128)S(1)} custom-call(f32[1,128,128]{2,1,0:T(8,128)S(1)} %get-tuple-element.51), custom_call_target="InvertDiagBlocksLowerTriangular" | custom-call | tf_op jit(solution)/shard_map/jit(cholesky)/cholesky | solution.py:60
  244.0 11.7 %cholesky.103 = f32[128,128]{1,0:T(8,128)S(1)} custom-call(f32[128,128]{1,0:T(8,128)S(1)} %convolution_subtract_fusion.1), custom_call_target="Cholesky" | custom-call | tf_op jit(solution)/shard_map/jit(cholesky)/cholesky | solution.py:60
  255.8 0.7 compare_reduce_fusion
  257.8 0.7 fusion.5
  258.6 4.1 %while.1 = (s32[]{:T(128)}, f32[256,256]{1,0:T(8,128)S(1)}, s32[2,2]{1,0:T(2,128)S(1)}, f32[2,128,128]{2,1,0:T(8,128)S(1)}, s32[]{:T(128)}) while((s32[]{:T(128)}, f32[256,256]{1,0:T(8,128)S(1)}, s32[2,2]{1,0:T(2,128)S(1)}, f32[2,128,128]{2,1,0:T(8,128)S(1)}, s32[]{:T(128)}) %tuple.32), condition=%wide.while_cond, body=%wide.while_body.sunk | while | flops 2 | bytes 131181 | solution.py:61
  259.3 1.3 bitcast_dynamic-update-slice_fusion.2
  261.4 1.3 bitcast_dynamic-update-slice_fusion.2
  262.7 19.7 %custom-call.16 = f32[2,128,128]{1,2,0:T(8,128)S(1)} custom-call(f32[2,128,128]{2,1,0:T(8,128)S(1)} %get-tuple-element.33), custom_call_target="InvertDiagBlocksLowerTriangular" | custom-call | tf_op jit(solution)/shard_map/jit(_solve_triangular)/triangular_solve | solution.py:61
  (35 shorter events, 4.8 us)
Async XLA Ops:
  7.2 128.8 %reduce-scatter.2.cloned.1.call-start = ((), (), s32[]{:S(2)}) async-start(), calls=%async_computation.1 | async-start | bytes 819200 | tf_op jit(solution)/shard_map/reduce_scatter | solution.py:52
  117.1 99.4 %all-gather.5.cloned.1.call-start = ((), (), s32[]{:S(2)}) async-start(), calls=%async_computation.2 | async-start | bytes 8650752 | tf_op jit(solution)/shard_map/all_gather | solution.py:58
  220.4 62.0 %copy-start = (f32[160,256]{1,0:T(8,128)S(1)}, f32[160,256]{1,0:T(8,128)}, u32[]{:S(2)}) copy-start(f32[160,256]{1,0:T(8,128)} %reduce-scatter.2.cloned.1.call-done) | copy-start | bytes 491524
Sparse Core Ops, SparseCore 0:
  117.2 18.7 reduce-scatter.1
  139.4 77.0 all-gather.4
